TPU v7x, 512 devices: a whole 4x8x8 slice. The times are simulated.
512 devices in a mesh: node: 128 (over z, y, core), feat: 4 (over x).
Axes of the slice: x: 4, y: 8, z: 8, core: 2. Of those that a mesh axis runs over, the one named last changes fastest.
Arguments:
- embed: bfloat16 [256, 131072], P('feat', 'node'), may hold values from -6 to 6
- tile_weight: bfloat16 [128, 135, 128, 128], P('node'), may hold values from -0.125 to 0.125
- tile_rows: int32 [128, 135], P('node'), may hold values from 0 to 7
- tile_cols: int32 [128, 135], P('node'), may hold values from 0 to 135, as said below
- send_rows: int32 [128, 128], P('node'), may hold values from 0 to 7
- src_local: int32 [65536], P('node'), may hold values from 0 to 1023
- dst_owner: int32 [65536, 1], P('node'), may hold values from 0 to 127; in each aligned block of 512 rows (0 to 511, 512 to 1023, ...) at most 8 rows name the same one
- dst_local: int32 [65536], P('node'), may hold values from 0 to 1023
- w_in: bfloat16 [256, 1024], P('feat'), may hold values from -0.375 to 0.375
- b_in: float32 [1024], replicated, may hold values from -4 to 4
- w_out: float32 [1024], replicated, may hold values from -0.1875 to 0.1875
Outputs:
- propagated: bfloat16 [256, 131072], P('feat', 'node')
- scores: float32 [65536], P('node')
Inputs may be any that keep to these rules, and one draw needn't show every extreme that they name: In each part, the entries of tile_cols below 8 are the numbers 0 to 7 once each, and tile_rows equals tile_cols at those tiles; the other 127 entries are 8 + p for every part p other than the part itself, once each. `dst_owner`: among the 512 queries of one part, at most 8 have the same destination part, and exactly 8 do for some destination part.
All inputs are finite; a program needn't handle non-finite values.
Results may differ from a plain program's by a relative error of at most 0.015.
Values may be sent and summed in bfloat16 or wider, within the bound.
A program may use at most 64 MiB of HBM per device.

v0:
```python
import jax
import jax.numpy as jnp
from jax import lax
from jax.sharding import PartitionSpec as P

HOPS = 2
TELEPORT = 0.1


def propagate(current, initial, weights, tile_row, tile_col, targets):
    channels, node_count = current.shape
    block_size = weights.shape[-1]
    block_count = node_count // block_size
    blocked = current.reshape(channels, block_count, block_size)
    outgoing = blocked[:, targets, :]
    incoming = lax.all_to_all(outgoing, "node", split_axis=1, concat_axis=1, tiled=True)
    sources = jnp.concatenate([blocked, incoming], axis=1)
    picked = sources[:, tile_col, :]
    products = jnp.einsum("ctj,tij->cti", picked, weights, preferred_element_type=jnp.float32)
    selector = (tile_row[None, :] == jnp.arange(block_count, dtype=jnp.int32)[:, None]).astype(
        jnp.float32
    )
    summed = jnp.einsum("rt,cti->cri", selector, products, precision=lax.Precision.HIGHEST)
    return ((1.0 - TELEPORT) * summed.reshape(channels, node_count) + TELEPORT * initial).astype(
        jnp.bfloat16
    )


def contract_rows(left_matrix, right_matrix):
    return lax.dot_general(
        left_matrix, right_matrix, (((0,), (0,)), ((), ())), preferred_element_type=jnp.float32
    )


def shards(
    embed,
    tile_weight,
    tile_rows,
    tile_cols,
    send_rows,
    src_local,
    dst_owner,
    dst_local,
    w_in,
    b_in,
    w_out,
):
    weights = tile_weight[0]
    tile_row = tile_rows[0]
    tile_col = tile_cols[0]
    targets = send_rows[0]
    initial = embed.astype(jnp.float32)
    current = embed
    for hop_index in range(HOPS):
        current = propagate(current, initial, weights, tile_row, tile_col, targets)
    part_count = lax.axis_size("node")
    queries = src_local.shape[0]
    capacity = max(2, 2 * queries // part_count)
    owners = dst_owner[:, 0]
    owner_hits = (owners[:, None] == jnp.arange(part_count, dtype=jnp.int32)[None, :]).astype(
        jnp.int32
    )
    slot_rank = jnp.sum(jnp.cumsum(owner_hits, axis=0) * owner_hits, axis=1) - 1
    requests = (
        jnp.zeros((part_count * capacity,), jnp.int32)
        .at[owners * capacity + slot_rank]
        .set(dst_local)
    )
    requests = requests.reshape(part_count, capacity)
    replies = lax.all_to_all(
        current[:, lax.all_to_all(requests, "node", split_axis=0, concat_axis=0, tiled=True)],
        "node",
        split_axis=1,
        concat_axis=1,
        tiled=True,
    )
    target_rows = replies[:, owners, slot_rank]
    source_rows = current[:, src_local]
    hadamard = (source_rows.astype(jnp.float32) * target_rows.astype(jnp.float32)).astype(
        jnp.bfloat16
    )
    partial_value = contract_rows(w_in, hadamard)
    hidden = lax.psum(partial_value.astype(jnp.bfloat16), "feat").astype(jnp.float32)
    active = jnp.maximum(hidden + b_in[:, None], 0.0)
    scores = jnp.dot(w_out, active, precision=lax.Precision.HIGHEST)
    return (current, scores)


def solution(mesh):
    placed = (
        P("feat", "node"),
        P("node", None, None, None),
        P("node", None),
        P("node", None),
        P("node", None),
        P("node"),
        P("node", None),
        P("node"),
        P("feat", None),
        P(),
        P(),
    )
    return jax.shard_map(
        shards,
        mesh=mesh,
        in_specs=placed,
        out_specs=(P("feat", "node"), P("node")),
        check_vma=False,
    )
```

profile of v0, /device:TPU:8, one launch (start us, length us, event | category | flops | bytes accessed | tf_op | source)
XLA Modules:
  0.0 273.8 jit_solution(4774526276266268185)
XLA Ops:
  8.8 2.2 gather_fusion
  11.0 17.5 %all-to-all-start = ((bf16[64,128,128]{2,0,1:T(8,128)(2,1)}), bf16[64,128,128]{2,0,1:T(8,128)(2,1)S(1)}, u32[]{:S(2)}, u32[]{:S(2)}) async-start(bf16[64,128,128]{2,0,1:T(8,128)(2,1)} %bitcast.90), calls=%async_computation | async-start | bytes 4194304 | tf_op jit(solution)/shard_map/all_to_all | solution.py:16
  29.4 2.6 scatter_custom_fusion
  32.7 49.8 %all-to-all-done = bf16[64,128,128]{2,0,1:T(8,128)(2,1)S(1)} async-done(((bf16[64,128,128]{2,0,1:T(8,128)(2,1)}), bf16[64,128,128]{2,0,1:T(8,128)(2,1)S(1)}, u32[]{:S(2)}, u32[]{:S(2)}) %all-to-all-start) | async-done | bytes 2097184 | tf_op jit(solution)/shard_map/all_to_all | solution.py:16
  82.5 6.1 %all-to-all-start.2 = ((s32[128,1,8]{2,1,0:T(1,128)}), s32[128,1,8]{2,1,0:T(1,128)S(1)}, u32[]{:S(2)}, u32[]{:S(2)}) async-start(s32[128,1,8]{2,1,0:T(1,128)} %bitcast.25), calls=%async_computation.2 | async-start | bytes 131072 | tf_op jit(solution)/shard_map/all_to_all | solution.py:71
  88.6 1.6 pad_maximum_fusion
  90.2 2.6 gather_fusion.1
  92.8 5.4 %fusion.10 = f32[64,135,128]{2,0,1:T(8,128)S(1)} fusion(bf16[1,135,128,128]{3,2,1,0:T(8,128)(2,1)} %param.12, bf16[135,64,128]{2,1,0:T(8,128)(2,1)S(1)} %gather_fusion.1), kind=kOutput, calls=%fused_computation.20 | convolution fusion | flops 283115520 | bytes 11059200 | tf_op jit(solution)/shard_map/ctj,tij->cti/dot_general | solution.py:19
  98.2 4.0 %fusion.34 = f32[64,8,128]{2,1,0:T(8,128)S(1)} fusion(f32[64,135,128]{2,0,1:T(8,128)S(1)} %fusion.10, s32[135]{0:T(256)S(1)} %bitcast.101), kind=kOutput, calls=%fused_computation.31 | convolution fusion | flops 106234936 | bytes 4686364 | tf_op jit(solution)/shard_map/rt,cti->cri/dot_general | solution.py:23
  102.7 2.2 gather_fusion.2
  104.8 13.7 %all-to-all-start.1 = ((bf16[64,128,128]{2,0,1:T(8,128)(2,1)}), bf16[64,128,128]{2,0,1:T(8,128)(2,1)S(1)}, u32[]{:S(2)}, u32[]{:S(2)}) async-start(bf16[64,128,128]{2,0,1:T(8,128)(2,1)} %bitcast.13), calls=%async_computation.1 | async-start | bytes 4194304 | tf_op jit(solution)/shard_map/all_to_all | solution.py:16
  118.7 53.9 %all-to-all-done.1 = bf16[64,128,128]{2,0,1:T(8,128)(2,1)S(1)} async-done(((bf16[64,128,128]{2,0,1:T(8,128)(2,1)}), bf16[64,128,128]{2,0,1:T(8,128)(2,1)S(1)}, u32[]{:S(2)}, u32[]{:S(2)}) %all-to-all-start.1) | async-done | bytes 2097184 | tf_op jit(solution)/shard_map/all_to_all | solution.py:16
  172.6 1.6 pad_maximum_fusion.1
  174.2 2.6 gather_fusion.3
  176.8 5.4 %fusion.15 = f32[64,135,128]{2,0,1:T(8,128)S(1)} fusion(bf16[1,135,128,128]{3,2,1,0:T(8,128)(2,1)} %param.12, bf16[135,64,128]{2,1,0:T(8,128)(2,1)S(1)} %gather_fusion.3), kind=kOutput, calls=%fused_computation.21 | convolution fusion | flops 283115520 | bytes 11059200 | tf_op jit(solution)/shard_map/ctj,tij->cti/dot_general | solution.py:19
  182.2 4.0 %fusion.31 = f32[64,8,128]{2,1,0:T(8,128)S(1)} fusion(f32[64,135,128]{2,0,1:T(8,128)S(1)} %fusion.15, s32[135]{0:T(256)S(1)} %bitcast.102), kind=kOutput, calls=%fused_computation.30 | convolution fusion | flops 106234936 | bytes 4686364 | tf_op jit(solution)/shard_map/rt,cti->cri/dot_general | solution.py:23
  186.5 3.2 %gather_fusion.5 = bf16[1024,64]{1,0:T(8,128)(2,1)S(1)} fusion(bf16[64,1024]{0,1:T(8,128)(2,1)S(1)} %fusion.39, s32[1024]{0:T(1024)S(1)} %broadcast_clamp_fusion), kind=kCustom, calls=%fused_computation.5 | custom fusion | bytes 266240 | tf_op jit(solution)/shard_map/gather | solution.py:71
  190.7 6.2 %all-to-all-start.3 = ((bf16[128,2,256]{2,1,0:T(2,128)(2,1)}), bf16[128,2,256]{2,1,0:T(2,128)(2,1)S(1)}, u32[]{:S(2)}, u32[]{:S(2)}) async-start(bf16[128,2,256]{2,1,0:T(2,128)(2,1)} %reshape.217), calls=%async_computation.3 | async-start | bytes 262144 | tf_op jit(solution)/shard_map/all_to_all | solution.py:70
  197.2 1.3 gather_fusion.4
  198.6 10.2 %all-to-all-done.3 = bf16[128,2,256]{2,1,0:T(2,128)(2,1)S(1)} async-done(((bf16[128,2,256]{2,1,0:T(2,128)(2,1)}), bf16[128,2,256]{2,1,0:T(2,128)(2,1)S(1)}, u32[]{:S(2)}, u32[]{:S(2)}) %all-to-all-start.3) | async-done | bytes 131104 | tf_op jit(solution)/shard_map/all_to_all | solution.py:70
  209.0 3.1 %gather_fusion.6 = bf16[512,64]{1,0:T(8,128)(2,1)S(1)} fusion(bf16[64,128,8]{0,2,1:T(8,128)(2,1)S(1)} %bitcast.91, s32[512]{0:T(512)S(1)} %bitcast.89), kind=kCustom, calls=%fused_computation.6 | custom fusion | bytes 135168 | tf_op jit(solution)/shard_map/gather | solution.py:77
  212.1 1.5 fusion.24
  214.4 48.7 %all-reduce.2.cloned.1.call-done = bf16[1024,512]{0,1:T(8,128)(2,1)} async-done(((bf16[1024,512]{0,1:T(8,128)(2,1)}), bf16[1024,512]{0,1:T(8,128)(2,1)}) %all-reduce.2.cloned.1.call-update) | async-done | bytes 1048592 | tf_op jit(solution)/shard_map/psum | solution.py:83
  263.1 3.9 %fusion.20 = f32[1,512]{1,0:T(1,128)} fusion(f32[1024,1]{0,1:T(1,128)S(1)} %bitcast.105, bf16[1024,512]{0,1:T(8,128)(2,1)} %all-reduce.2.cloned.1.call-done, f32[1024]{0:T(1024)S(1)} %copy-done.7), kind=kOutput, calls=%fused_computation.22 | convolution fusion | flops 7864320 | bytes 1058816 | tf_op jit(solution)/shard_map/dot_general | solution.py:85
  (51 shorter events, 6.3 us)
Async XLA Ops:
  7.2 204.9 %copy-start = (bf16[64,1024]{1,0:T(8,128)(2,1)S(1)}, bf16[64,1024]{1,0:T(8,128)(2,1)}, u32[]{:S(2)}) copy-start(bf16[64,1024]{1,0:T(8,128)(2,1)} %param.19) | copy-start | bytes 393220
  11.0 17.5 %copy-start.1 = (bf16[64,1024]{1,0:T(8,128)(2,1)S(1)}, bf16[64,1024]{1,0:T(8,128)(2,1)}, u32[]{:S(2)}) copy-start(bf16[64,1024]{1,0:T(8,128)(2,1)} %param.11) | copy-start | bytes 393220
  11.0 17.7 %copy-start.2 = (s32[512,1]{0,1:T(1,128)S(1)}, s32[512,1]{0,1:T(1,128)}, u32[]{:S(2)}) copy-start(s32[512,1]{0,1:T(1,128)} %param.17) | copy-start | bytes 6148
  11.0 21.7 %copy-start.5 = (s32[1,135]{1,0:T(1,128)S(1)}, s32[1,135]{1,0:T(1,128)}, u32[]{:S(2)}) copy-start(s32[1,135]{1,0:T(1,128)} %param.14) | copy-start | bytes 1624
  11.0 71.6 %all-to-all-start = ((bf16[64,128,128]{2,0,1:T(8,128)(2,1)}), bf16[64,128,128]{2,0,1:T(8,128)(2,1)S(1)}, u32[]{:S(2)}, u32[]{:S(2)}) async-start(bf16[64,128,128]{2,0,1:T(8,128)(2,1)} %bitcast.90), calls=%async_computation | async-start | bytes 4194304 | tf_op jit(solution)/shard_map/all_to_all | solution.py:16
  82.5 22.3 %all-to-all-start.2 = ((s32[128,1,8]{2,1,0:T(1,128)}), s32[128,1,8]{2,1,0:T(1,128)S(1)}, u32[]{:S(2)}, u32[]{:S(2)}) async-start(s32[128,1,8]{2,1,0:T(1,128)} %bitcast.25), calls=%async_computation.2 | async-start | bytes 131072 | tf_op jit(solution)/shard_map/all_to_all | solution.py:71
  92.8 5.4 %copy-start.3 = (s32[1,135]{1,0:T(1,128)S(1)}, s32[1,135]{1,0:T(1,128)}, u32[]{:S(2)}) copy-start(s32[1,135]{1,0:T(1,128)} %param.13) | copy-start | bytes 1624
  104.8 67.8 %all-to-all-start.1 = ((bf16[64,128,128]{2,0,1:T(8,128)(2,1)}), bf16[64,128,128]{2,0,1:T(8,128)(2,1)S(1)}, u32[]{:S(2)}, u32[]{:S(2)}) async-start(bf16[64,128,128]{2,0,1:T(8,128)(2,1)} %bitcast.13), calls=%async_computation.1 | async-start | bytes 4194304 | tf_op jit(solution)/shard_map/all_to_all | solution.py:16
  186.5 10.6 %copy-start.4 = (s32[512]{0:T(512)S(1)}, s32[512]{0:T(512)}, u32[]{:S(2)}) copy-start(s32[512]{0:T(512)} %param.16) | copy-start | bytes 6148
  190.7 18.1 %all-to-all-start.3 = ((bf16[128,2,256]{2,1,0:T(2,128)(2,1)}), bf16[128,2,256]{2,1,0:T(2,128)(2,1)S(1)}, u32[]{:S(2)}, u32[]{:S(2)}) async-start(bf16[128,2,256]{2,1,0:T(2,128)(2,1)} %reshape.217), calls=%async_computation.3 | async-start | bytes 262144 | tf_op jit(solution)/shard_map/all_to_all | solution.py:70
  196.8 66.2 %all-reduce.2.cloned.1.call-start = ((), (), s32[]{:S(2)}) async-start(), calls=%async_computation.4 | async-start | bytes 2097152 | tf_op jit(solution)/shard_map/psum | solution.py:83
  198.5 64.6 %copy-start.6 = (f32[1024]{0:T(1024)S(1)}, f32[1024]{0:T(1024)}, u32[]{:S(2)}) copy-start(f32[1024]{0:T(1024)} %param.21) | copy-start | bytes 12292
  198.5 64.5 %copy-start.7 = (f32[1024]{0:T(1024)S(1)}, f32[1024]{0:T(1024)}, u32[]{:S(2)}) copy-start(f32[1024]{0:T(1024)} %param.20) | copy-start | bytes 12292
Sparse Core Ops, SparseCore 0:
  213.7 49.3 all-reduce.1
where the time goes:
time: 274 us
  waiting for transfers between devices  163 us (59%)
  starting transfers between devices  43.8 us (16%)
  local copies, waits for them, and re-layouts  24.4 us (9%)
  matrix products  24.1 us (9%)
  between operations  14.3 us (5%)
  other arithmetic  4.5 us (2%)
    all_to_all x2, waiting for transfers between devices, propagate(): lax.all_to_all(outgoing, 'node', split_axis=1, concat_axis=1, tiled=True)  104 us
    psum x1, waiting for transfers between devices, shards(): lax.psum(partial_value.astype(jnp.bfloat16), 'feat').astype(jnp.float32)  48.7 us
    all_to_all x2, starting transfers between devices, propagate(): lax.all_to_all(outgoing, 'node', split_axis=1, concat_axis=1, tiled=True)  31.2 us
    dot_general x2, matrix products, propagate(): jnp.einsum('ctj,tij->cti', picked, weights, preferred_element_type=jnp.fl...  10.8 us
    all_to_all x1, waiting for transfers between devices, shards(): lax.all_to_all(current[:, lax.all_to_all(requests, 'node', split_axis=0,...  10.2 us
    dot_general x2, matrix products, propagate(): jnp.einsum('rt,cti->cri', selector, products, precision=lax.Precision.HIG...  7.96 us
    all_to_all x1, starting transfers between devices, shards(): lax.all_to_all(current[:, lax.all_to_all(requests, 'node', split_axis=0,...  6.16 us
    all_to_all x1, starting transfers between devices, shards(): lax.all_to_all(requests, 'node', split_axis=0, concat_axis=0, tiled=True)  6.07 us
  transfers between devices with their start and end apart: 5, of which 4 were waited for; matrix products, arithmetic and copies ran while one was open for 8% of the time, Pallas kernels for 0%

commit v1 on v0

--- a/solution.py
+++ b/solution.py
@@ -80,7 +80,9 @@
         jnp.bfloat16
     )
     partial_value = contract_rows(w_in, hadamard)
-    hidden = lax.psum(partial_value.astype(jnp.bfloat16), "feat").astype(jnp.float32)
+    hidden = jnp.sum(lax.all_gather(partial_value.astype(jnp.bfloat16), "feat"), axis=0).astype(
+        jnp.float32
+    )
     active = jnp.maximum(hidden + b_in[:, None], 0.0)
     scores = jnp.dot(w_out, active, precision=lax.Precision.HIGHEST)
     return (current, scores)

time: 274 us -> 286 us (1.044)
  the two profiles are of different devices: /device:TPU:8 before, /device:TPU:1 now
where the time goes in v1:
time: 286 us
  waiting for transfers between devices  154 us (54%)
  starting transfers between devices  50.4 us (18%)
  local copies, waits for them, and re-layouts  32.2 us (11%)
  matrix products  22.8 us (8%)
  between operations  14.3 us (5%)
  other arithmetic  11.8 us (4%)
    all_to_all x2, waiting for transfers between devices, propagate(): lax.all_to_all(outgoing, 'node', split_axis=1, concat_axis=1, tiled=True)  98.2 us
    all_gather x1, waiting for transfers between devices, shards(): lax.all_gather(partial_value.astype(jnp.bfloat16), 'feat')  44.9 us
    all_to_all x2, starting transfers between devices, propagate(): lax.all_to_all(outgoing, 'node', split_axis=1, concat_axis=1, tiled=True)  32.3 us
    all_to_all x1, waiting for transfers between devices, shards(): lax.all_to_all(current[:, lax.all_to_all(requests, 'node', split_axis=0,...  11 us
    dot_general x2, matrix products, propagate(): jnp.einsum('ctj,tij->cti', picked, weights, preferred_element_type=jnp.fl...  10.8 us
    all_to_all x1, starting transfers between devices, shards(): lax.all_to_all(current[:, lax.all_to_all(requests, 'node', split_axis=0,...  8.95 us
    all_to_all x1, starting transfers between devices, shards(): lax.all_to_all(requests, 'node', split_axis=0, concat_axis=0, tiled=True)  8.85 us
    dot_general x2, matrix products, propagate(): jnp.einsum('rt,cti->cri', selector, products, precision=lax.Precision.HIG...  7.96 us
  transfers between devices with their start and end apart: 5, of which 4 were waited for; matrix products, arithmetic and copies ran while one was open for 8% of the time, Pallas kernels for 0%

profile of v1, /device:TPU:1, one launch (start us, length us, event | category | flops | bytes accessed | tf_op | source)
XLA Modules:
  0.0 285.6 jit_solution(9460009023067622506)
XLA Ops:
  8.8 2.2 gather_fusion
  11.0 18.6 %all-to-all-start = ((bf16[64,128,128]{2,0,1:T(8,128)(2,1)}), bf16[64,128,128]{2,0,1:T(8,128)(2,1)S(1)}, u32[]{:S(2)}, u32[]{:S(2)}) async-start(bf16[64,128,128]{2,0,1:T(8,128)(2,1)} %bitcast.93), calls=%async_computation | async-start | bytes 4194304 | tf_op jit(solution)/shard_map/all_to_all | solution.py:16
  30.4 2.6 scatter_custom_fusion
  33.8 47.0 %all-to-all-done = bf16[64,128,128]{2,0,1:T(8,128)(2,1)S(1)} async-done(((bf16[64,128,128]{2,0,1:T(8,128)(2,1)}), bf16[64,128,128]{2,0,1:T(8,128)(2,1)S(1)}, u32[]{:S(2)}, u32[]{:S(2)}) %all-to-all-start) | async-done | bytes 2097184 | tf_op jit(solution)/shard_map/all_to_all | solution.py:16
  80.8 8.9 %all-to-all-start.2 = ((s32[128,1,8]{2,1,0:T(1,128)}), s32[128,1,8]{2,1,0:T(1,128)S(1)}, u32[]{:S(2)}, u32[]{:S(2)}) async-start(s32[128,1,8]{2,1,0:T(1,128)} %bitcast.25), calls=%async_computation.2 | async-start | bytes 131072 | tf_op jit(solution)/shard_map/all_to_all | solution.py:71
  89.7 1.6 pad_maximum_fusion
  91.2 2.6 gather_fusion.1
  93.9 5.4 %fusion.10 = f32[64,135,128]{2,0,1:T(8,128)S(1)} fusion(bf16[1,135,128,128]{3,2,1,0:T(8,128)(2,1)} %param.12, bf16[135,64,128]{2,1,0:T(8,128)(2,1)S(1)} %gather_fusion.1), kind=kOutput, calls=%fused_computation.20 | convolution fusion | flops 283115520 | bytes 11059200 | tf_op jit(solution)/shard_map/ctj,tij->cti/dot_general | solution.py:19
  99.3 4.0 %fusion.34 = f32[64,8,128]{2,1,0:T(8,128)S(1)} fusion(f32[64,135,128]{2,0,1:T(8,128)S(1)} %fusion.10, s32[135]{0:T(256)S(1)} %bitcast.104), kind=kOutput, calls=%fused_computation.31 | convolution fusion | flops 106234936 | bytes 4686364 | tf_op jit(solution)/shard_map/rt,cti->cri/dot_general | solution.py:23
  103.7 2.2 gather_fusion.2
  105.9 13.7 %all-to-all-start.1 = ((bf16[64,128,128]{2,0,1:T(8,128)(2,1)}), bf16[64,128,128]{2,0,1:T(8,128)(2,1)S(1)}, u32[]{:S(2)}, u32[]{:S(2)}) async-start(bf16[64,128,128]{2,0,1:T(8,128)(2,1)} %bitcast.13), calls=%async_computation.1 | async-start | bytes 4194304 | tf_op jit(solution)/shard_map/all_to_all | solution.py:16
  119.8 51.1 %all-to-all-done.1 = bf16[64,128,128]{2,0,1:T(8,128)(2,1)S(1)} async-done(((bf16[64,128,128]{2,0,1:T(8,128)(2,1)}), bf16[64,128,128]{2,0,1:T(8,128)(2,1)S(1)}, u32[]{:S(2)}, u32[]{:S(2)}) %all-to-all-start.1) | async-done | bytes 2097184 | tf_op jit(solution)/shard_map/all_to_all | solution.py:16
  170.9 1.6 pad_maximum_fusion.1
  172.5 2.6 gather_fusion.3
  175.1 5.4 %fusion.15 = f32[64,135,128]{2,0,1:T(8,128)S(1)} fusion(bf16[1,135,128,128]{3,2,1,0:T(8,128)(2,1)} %param.12, bf16[135,64,128]{2,1,0:T(8,128)(2,1)S(1)} %gather_fusion.3), kind=kOutput, calls=%fused_computation.21 | convolution fusion | flops 283115520 | bytes 11059200 | tf_op jit(solution)/shard_map/ctj,tij->cti/dot_general | solution.py:19
  180.5 4.0 %fusion.31 = f32[64,8,128]{2,1,0:T(8,128)S(1)} fusion(f32[64,135,128]{2,0,1:T(8,128)S(1)} %fusion.15, s32[135]{0:T(256)S(1)} %bitcast.105), kind=kOutput, calls=%fused_computation.30 | convolution fusion | flops 106234936 | bytes 4686364 | tf_op jit(solution)/shard_map/rt,cti->cri/dot_general | solution.py:23
  184.8 3.2 %gather_fusion.5 = bf16[1024,64]{1,0:T(8,128)(2,1)S(1)} fusion(bf16[64,1024]{0,1:T(8,128)(2,1)S(1)} %fusion.39, s32[1024]{0:T(1024)S(1)} %broadcast_clamp_fusion), kind=kCustom, calls=%fused_computation.5 | custom fusion | bytes 266240 | tf_op jit(solution)/shard_map/gather | solution.py:71
  188.9 8.9 %all-to-all-start.3 = ((bf16[128,2,256]{2,1,0:T(2,128)(2,1)}), bf16[128,2,256]{2,1,0:T(2,128)(2,1)S(1)}, u32[]{:S(2)}, u32[]{:S(2)}) async-start(bf16[128,2,256]{2,1,0:T(2,128)(2,1)} %reshape.218), calls=%async_computation.3 | async-start | bytes 262144 | tf_op jit(solution)/shard_map/all_to_all | solution.py:70
  199.6 11.0 %all-to-all-done.3 = bf16[128,2,256]{2,1,0:T(2,128)(2,1)S(1)} async-done(((bf16[128,2,256]{2,1,0:T(2,128)(2,1)}), bf16[128,2,256]{2,1,0:T(2,128)(2,1)S(1)}, u32[]{:S(2)}, u32[]{:S(2)}) %all-to-all-start.3) | async-done | bytes 131104 | tf_op jit(solution)/shard_map/all_to_all | solution.py:70
  210.8 3.1 %gather_fusion.6 = bf16[512,64]{1,0:T(8,128)(2,1)S(1)} fusion(bf16[64,128,8]{0,2,1:T(8,128)(2,1)S(1)} %bitcast.94, s32[512]{0:T(512)S(1)} %bitcast.92), kind=kCustom, calls=%fused_computation.6 | custom fusion | bytes 135168 | tf_op jit(solution)/shard_map/gather | solution.py:77
  216.1 44.9 %all-gather.3.cloned.1.call-done = bf16[4096,512]{0,1:T(8,128)(2,1)} async-done(((bf16[1024,512]{0,1:T(8,128)(2,1)}), bf16[4096,512]{0,1:T(8,128)(2,1)}) %all-gather.3.cloned.1.call-update) | async-done | bytes 4194320 | tf_op jit(solution)/shard_map/all_gather | solution.py:83
  261.0 7.9 %reshape.210 = bf16[4,1024,512]{1,0,2:T(4,128)(2,1)} reshape(bf16[4096,512]{0,1:T(8,128)(2,1)} %all-gather.3.cloned.1.call-done) | data formatting | bytes 8388608 | tf_op jit(solution)/shard_map/all_gather | solution.py:83
  268.8 7.3 %reduce_sum.22 = bf16[1024,512]{0,1:T(8,128)(2,1)S(1)} reduce(bf16[4,1024,512]{1,0,2:T(4,128)(2,1)} %reshape.210, bf16[]{:T(256)} %constant.8.clone.1), dimensions={0}, to_apply=%region_4.5 | reduce | flops 1572864 | bytes 5242882 | tf_op jit(solution)/shard_map/reduce_sum | solution.py:83
  276.1 2.6 fusion.20
  (53 shorter events, 9.0 us)
Async XLA Ops:
  7.2 206.7 %copy-start = (bf16[64,1024]{1,0:T(8,128)(2,1)S(1)}, bf16[64,1024]{1,0:T(8,128)(2,1)}, u32[]{:S(2)}) copy-start(bf16[64,1024]{1,0:T(8,128)(2,1)} %param.19) | copy-start | bytes 393220
  11.0 18.6 %copy-start.1 = (bf16[64,1024]{1,0:T(8,128)(2,1)S(1)}, bf16[64,1024]{1,0:T(8,128)(2,1)}, u32[]{:S(2)}) copy-start(bf16[64,1024]{1,0:T(8,128)(2,1)} %param.11) | copy-start | bytes 393220
  11.0 18.7 %copy-start.2 = (s32[512,1]{0,1:T(1,128)S(1)}, s32[512,1]{0,1:T(1,128)}, u32[]{:S(2)}) copy-start(s32[512,1]{0,1:T(1,128)} %param.17) | copy-start | bytes 6148
  11.0 22.8 %copy-start.5 = (s32[1,135]{1,0:T(1,128)S(1)}, s32[1,135]{1,0:T(1,128)}, u32[]{:S(2)}) copy-start(s32[1,135]{1,0:T(1,128)} %param.14) | copy-start | bytes 1624
  11.0 69.8 %all-to-all-start = ((bf16[64,128,128]{2,0,1:T(8,128)(2,1)}), bf16[64,128,128]{2,0,1:T(8,128)(2,1)S(1)}, u32[]{:S(2)}, u32[]{:S(2)}) async-start(bf16[64,128,128]{2,0,1:T(8,128)(2,1)} %bitcast.93), calls=%async_computation | async-start | bytes 4194304 | tf_op jit(solution)/shard_map/all_to_all | solution.py:16
  80.8 25.1 %all-to-all-start.2 = ((s32[128,1,8]{2,1,0:T(1,128)}), s32[128,1,8]{2,1,0:T(1,128)S(1)}, u32[]{:S(2)}, u32[]{:S(2)}) async-start(s32[128,1,8]{2,1,0:T(1,128)} %bitcast.25), calls=%async_computation.2 | async-start | bytes 131072 | tf_op jit(solution)/shard_map/all_to_all | solution.py:71
  93.9 5.4 %copy-start.3 = (s32[1,135]{1,0:T(1,128)S(1)}, s32[1,135]{1,0:T(1,128)}, u32[]{:S(2)}) copy-start(s32[1,135]{1,0:T(1,128)} %param.13) | copy-start | bytes 1624
  105.9 65.0 %all-to-all-start.1 = ((bf16[64,128,128]{2,0,1:T(8,128)(2,1)}), bf16[64,128,128]{2,0,1:T(8,128)(2,1)S(1)}, u32[]{:S(2)}, u32[]{:S(2)}) async-start(bf16[64,128,128]{2,0,1:T(8,128)(2,1)} %bitcast.13), calls=%async_computation.1 | async-start | bytes 4194304 | tf_op jit(solution)/shard_map/all_to_all | solution.py:16
  184.8 13.4 %copy-start.4 = (s32[512]{0:T(512)S(1)}, s32[512]{0:T(512)}, u32[]{:S(2)}) copy-start(s32[512]{0:T(512)} %param.16) | copy-start | bytes 6148
  188.9 21.7 %all-to-all-start.3 = ((bf16[128,2,256]{2,1,0:T(2,128)(2,1)}), bf16[128,2,256]{2,1,0:T(2,128)(2,1)S(1)}, u32[]{:S(2)}, u32[]{:S(2)}) async-start(bf16[128,2,256]{2,1,0:T(2,128)(2,1)} %reshape.218), calls=%async_computation.3 | async-start | bytes 262144 | tf_op jit(solution)/shard_map/all_to_all | solution.py:70
  197.9 63.1 %all-gather.3.cloned.1.call-start = ((), (), s32[]{:S(2)}) async-start(), calls=%async_computation.4 | async-start | bytes 5242880 | tf_op jit(solution)/shard_map/all_gather | solution.py:83
  268.8 7.3 %copy-start.6 = (f32[1024]{0:T(1024)S(1)}, f32[1024]{0:T(1024)}, u32[]{:S(2)}) copy-start(f32[1024]{0:T(1024)} %param.21) | copy-start | bytes 12292
  268.8 7.3 %copy-start.7 = (f32[1024]{0:T(1024)S(1)}, f32[1024]{0:T(1024)}, u32[]{:S(2)}) copy-start(f32[1024]{0:T(1024)} %param.20) | copy-start | bytes 12292
Sparse Core Ops, SparseCore 0:
  215.4 45.4 all-gather.2
